TPU v7x, 32 devices: a whole 2x2x4 slice. The times are simulated.
32 devices in a mesh: dp: 4 (over x, core), row: 4 (over z), col: 2 (over y).
Axes of the slice: x: 2, y: 2, z: 4, core: 2. Of those that a mesh axis runs over, the one named last changes fastest.
Arguments:
- tokens_in: bfloat16 [8192, 768], P(('dp', 'col'), 'row'), may hold values from -6 to 6
- out_cot: bfloat16 [8192, 768], P(('dp', 'col'), 'row'), may hold values from -6 to 6
- segments: int32 [16, 512], P('dp'), may hold values from 0 to 31, never falling along the last dimension, each value on 1 to 256 neighbouring positions
- norm_params: float32 [4, 768], P(None, 'row'), may hold values from -1.2 to 1.5, as said below
- qkv_weight: float32 [768, 2304], P('row', 'col'), may hold values from -0.21875 to 0.21875
- proj_weight: float32 [768, 768], P('col', 'row'), may hold values from -0.875 to 0.875
- up_weight: float32 [768, 3072], P('row', 'col'), may hold values from -0.21875 to 0.21875
- down_weight: float32 [3072, 768], P('col', 'row'), may hold values from -0.109375 to 0.109375
- norm_first: float32 [4, 768], P(None, 'row'), may hold values from -18 to 18
- norm_second: float32 [4, 768], P(None, 'row'), may hold values from 30 to 300
- qkv_first: float32 [768, 2304], P('row', 'col'), may hold values from -18 to 18
- qkv_second: float32 [768, 2304], P('row', 'col'), may hold values from 30 to 300
- proj_first: float32 [768, 768], P('col', 'row'), may hold values from -18 to 18
- proj_second: float32 [768, 768], P('col', 'row'), may hold values from 30 to 300
- up_first: float32 [768, 3072], P('row', 'col'), may hold values from -18 to 18
- up_second: float32 [768, 3072], P('row', 'col'), may hold values from 30 to 300
- down_first: float32 [3072, 768], P('col', 'row'), may hold values from -18 to 18
- down_second: float32 [3072, 768], P('col', 'row'), may hold values from 30 to 300
Outputs:
- output: bfloat16 [8192, 768], P(('dp', 'col'), 'row')
- input_grad: bfloat16 [8192, 768], P(('dp', 'col'), 'row')
- norm_grad: float32 [4, 768], P(None, 'row')
- qkv_grad: float32 [768, 2304], P('row', 'col')
- proj_grad: float32 [768, 768], P('col', 'row')
- up_grad: float32 [768, 3072], P('row', 'col')
- down_grad: float32 [3072, 768], P('col', 'row')
- norm_new: float32 [4, 768], P(None, 'row')
- qkv_new: float32 [768, 2304], P('row', 'col')
- proj_new: float32 [768, 768], P('col', 'row')
- up_new: float32 [768, 3072], P('row', 'col')
- down_new: float32 [3072, 768], P('col', 'row')
- norm_first_new: float32 [4, 768], P(None, 'row')
- norm_second_new: float32 [4, 768], P(None, 'row')
- qkv_first_new: float32 [768, 2304], P('row', 'col')
- qkv_second_new: float32 [768, 2304], P('row', 'col')
- proj_first_new: float32 [768, 768], P('col', 'row')
- proj_second_new: float32 [768, 768], P('col', 'row')
- up_first_new: float32 [768, 3072], P('row', 'col')
- up_second_new: float32 [768, 3072], P('row', 'col')
- down_first_new: float32 [3072, 768], P('col', 'row')
- down_second_new: float32 [3072, 768], P('col', 'row')
Inputs may be any that keep to these rules, and one draw needn't show every extreme that they name: `segments`: within a row the numbers never fall; no number covers more than 256 positions of a row, and one covers exactly that many. `norm_params`: rows 0 and 2 lie in 0.5 to 1.5.
All inputs are finite; a program needn't handle non-finite values.
Results may differ from a plain program's by a relative error of at most 0.0093.
Values may be sent and summed in bfloat16 or wider, within the bound.
A program may use at most 192 MiB of HBM per device.

v0:
```python
import math
import jax
import jax.numpy as jnp
from jax import lax
from jax.sharding import PartitionSpec as P

D = 768
HEAD_DIM = 64
ROT_DIM = 16
SEQ_LEN = 512
STEP = 3
norm_eps = 1e-05
rotary_base = 10000.0
learn_rate = 0.01
beta_first = 0.9
beta_second = 0.95
adam_eps = 1e-08
decay_rate = 0.1
mask_fill = -1e30
inv_sqrt_two = 0.7071067811865476
inv_sqrt_two_pi = 0.3989422804014327


def gelu_value(value):
    return 0.5 * value * (1.0 + lax.erf(value * inv_sqrt_two))


def gelu_slope(value):
    return 0.5 * (1.0 + lax.erf(value * inv_sqrt_two)) + value * inv_sqrt_two_pi * jnp.exp(
        -0.5 * value * value
    )


def positions_of(segs):
    length = segs.shape[-1]
    index = jnp.broadcast_to(jnp.arange(length, dtype=jnp.int32), segs.shape)
    starts = jnp.concatenate(
        [jnp.ones(segs.shape[:-1] + (1,), bool), segs[..., 1:] != segs[..., :-1]], -1
    )
    first = lax.cummax(jnp.where(starts, index, 0), axis=segs.ndim - 1)
    return index - first


def rotary_tables(positions):
    half = ROT_DIM // 2
    freq = rotary_base ** (-2.0 * jnp.arange(half, dtype=jnp.float32) / ROT_DIM)
    angle = positions.astype(jnp.float32)[..., None] * freq
    return (jnp.cos(angle), jnp.sin(angle))


def rotate(tensor, cosine, sine):
    half = ROT_DIM // 2
    cos_part = cosine[..., None, :]
    sin_part = sine[..., None, :]
    front = tensor[..., :half]
    back = tensor[..., half:ROT_DIM]
    return jnp.concatenate(
        [
            front * cos_part - back * sin_part,
            back * cos_part + front * sin_part,
            tensor[..., ROT_DIM:],
        ],
        -1,
    )


def rotate_back(grad, cosine, sine):
    half = ROT_DIM // 2
    cos_part = cosine[..., None, :]
    sin_part = sine[..., None, :]
    front = grad[..., :half]
    back = grad[..., half:ROT_DIM]
    return jnp.concatenate(
        [
            front * cos_part + back * sin_part,
            back * cos_part - front * sin_part,
            grad[..., ROT_DIM:],
        ],
        -1,
    )


def masked_scores(query, keys, segment):
    length = segment.shape[0]
    scores = jnp.einsum(
        "qhd,khd->hqk", query, keys, preferred_element_type=jnp.float32
    ) / math.sqrt(HEAD_DIM)
    index = jnp.arange(length, dtype=jnp.int32)
    allowed = (segment[:, None] == segment[None, :]) & (index[None, :] <= index[:, None])
    return jnp.where(allowed[None], scores, mask_fill)


def attend(query, keys, values, segment):
    scores = masked_scores(query, keys, segment)
    total = jnp.sum(jnp.exp(scores), -1, keepdims=True)
    logsum = jnp.log(total)
    weights = jnp.exp(scores - logsum).astype(jnp.bfloat16)
    mixed = jnp.einsum("hqk,khd->qhd", weights, values, preferred_element_type=jnp.float32).astype(
        jnp.bfloat16
    )
    return (mixed, logsum[..., 0])


def attend_back(query, keys, values, segment, logsum, mixed, grad_mixed):
    scores = masked_scores(query, keys, segment)
    probs = jnp.exp(scores - logsum[..., None])
    weights = probs.astype(jnp.bfloat16)
    value_grad = jnp.einsum("hqk,qhd->khd", weights, grad_mixed, preferred_element_type=jnp.float32)
    prod_grad = jnp.einsum("qhd,khd->hqk", grad_mixed, values, preferred_element_type=jnp.float32)
    delta = jnp.sum(grad_mixed.astype(jnp.float32) * mixed.astype(jnp.float32), -1).T
    score_grad = (probs * (prod_grad - delta[..., None]) / math.sqrt(HEAD_DIM)).astype(jnp.bfloat16)
    query_grad = jnp.einsum("hqk,khd->qhd", score_grad, keys, preferred_element_type=jnp.float32)
    key_grad = jnp.einsum("hqk,qhd->khd", score_grad, query, preferred_element_type=jnp.float32)
    return (query_grad, key_grad, value_grad)


def dot32(left, right):
    return jnp.dot(left, right, preferred_element_type=jnp.float32)


def dot_rows(left, right):
    return lax.dot_general(
        left, right, (((0,), (0,)), ((), ())), preferred_element_type=jnp.float32
    )


def dot_cols(left, right):
    return lax.dot_general(
        left, right, (((1,), (1,)), ((), ())), preferred_element_type=jnp.float32
    )


def adam_update(weight, first, second, grad, decay):
    first_new = beta_first * first + (1.0 - beta_first) * grad
    second_new = beta_second * second + (1.0 - beta_second) * grad * grad
    first_hat = first_new / (1.0 - beta_first**STEP)
    second_hat = second_new / (1.0 - beta_second**STEP)
    weight_new = weight - learn_rate * (
        first_hat / (jnp.sqrt(second_hat) + adam_eps) + decay * weight
    )
    return (weight_new, first_new, second_new)


def on_device(
    tokens_in,
    out_cot,
    segments,
    norm_params,
    qkv_weight,
    proj_weight,
    up_weight,
    down_weight,
    norm_first,
    norm_second,
    qkv_first,
    qkv_second,
    proj_first,
    proj_second,
    up_first,
    up_second,
    down_first,
    down_second,
):
    row_count = lax.axis_size("row")
    row_index = lax.axis_index("row")
    col_index = lax.axis_index("col")
    local_count = tokens_in.shape[0]
    heads_here = qkv_weight.shape[1] // (3 * HEAD_DIM)
    seq_count = segments.shape[0] // row_count
    x_all, cot_all = (
        lax.all_gather(tokens_in, "col", axis=0, tiled=True),
        lax.all_gather(out_cot, "col", axis=0, tiled=True),
    )
    group_count = x_all.shape[0]
    share = group_count // row_count
    xfull = x_all.astype(jnp.float32)
    sums = lax.psum((jnp.sum(xfull, 1), jnp.sum(xfull * xfull, 1)), "row")
    mean = sums[0] / D
    spread = sums[1] / D - mean * mean
    rstd = lax.rsqrt(spread + norm_eps)[:, None]
    normed = (xfull - mean[:, None]) * rstd
    first_in = (normed * norm_params[0] + norm_params[1]).astype(jnp.bfloat16)
    second_in = (normed * norm_params[2] + norm_params[3]).astype(jnp.bfloat16)
    qkv16 = qkv_weight.astype(jnp.bfloat16)
    up16 = up_weight.astype(jnp.bfloat16)
    proj_cat = jnp.concatenate(
        [proj_weight.astype(jnp.bfloat16), down_weight.astype(jnp.bfloat16)], 0
    )
    width_qkv = qkv16.shape[1]
    mixed_in = lax.psum_scatter(
        jnp.concatenate([dot32(first_in, qkv16), dot32(second_in, up16)], 1),
        "row",
        scatter_dimension=0,
        tiled=True,
    )
    qkv_own = mixed_in[:, :width_qkv]
    hidden_here = mixed_in[:, width_qkv:]
    seg_own = lax.dynamic_slice_in_dim(segments, row_index * seq_count, seq_count, 0)
    cosine, sine = rotary_tables(positions_of(seg_own))
    packed = qkv_own.reshape(seq_count, SEQ_LEN, heads_here, 3, HEAD_DIM)
    query = rotate(packed[..., 0, :], cosine, sine).astype(jnp.bfloat16)
    keys = rotate(packed[..., 1, :], cosine, sine).astype(jnp.bfloat16)
    values = packed[..., 2, :].astype(jnp.bfloat16)
    attended, logsum = lax.map(lambda item: attend(*item), (query, keys, values, seg_own))
    attn_width = heads_here * HEAD_DIM
    attn_flat = attended.reshape(share, attn_width)
    active = gelu_value(hidden_here).astype(jnp.bfloat16)
    attn_all, active_all = (
        lax.all_gather(attn_flat, "row", axis=0, tiled=True),
        lax.all_gather(active, "row", axis=0, tiled=True),
    )
    act_cat = jnp.concatenate([attn_all, active_all], 1)
    mixed_out = lax.psum_scatter(dot32(act_cat, proj_cat), "col", scatter_dimension=0, tiled=True)
    output = (tokens_in.astype(jnp.float32) + mixed_out).astype(jnp.bfloat16)
    grad_cat = dot_rows(act_cat, cot_all)
    act_grad = lax.psum_scatter(dot_cols(cot_all, proj_cat), "row", scatter_dimension=0, tiled=True)
    attended_grad = act_grad[:, :attn_width].astype(jnp.bfloat16)
    hidden_grad = (act_grad[:, attn_width:] * gelu_slope(hidden_here)).astype(jnp.bfloat16)
    grad_heads = attended_grad.reshape(seq_count, SEQ_LEN, heads_here, HEAD_DIM)
    query_grad, key_grad, value_grad = lax.map(
        lambda item: attend_back(*item),
        (query, keys, values, seg_own, logsum, attended, grad_heads),
    )
    query_grad = rotate_back(query_grad, cosine, sine)
    key_grad = rotate_back(key_grad, cosine, sine)
    packed_grad = (
        jnp.stack([query_grad, key_grad, value_grad], 3)
        .reshape(share, width_qkv)
        .astype(jnp.bfloat16)
    )
    packed_all, hidden_all = (
        lax.all_gather(packed_grad, "row", axis=0, tiled=True),
        lax.all_gather(hidden_grad, "row", axis=0, tiled=True),
    )
    qkv_grad = dot_rows(first_in, packed_all)
    up_grad = dot_rows(second_in, hidden_all)
    feature_count = first_in.shape[1]
    norm_in_grad = lax.psum(
        jnp.concatenate([dot_cols(packed_all, qkv16), dot_cols(hidden_all, up16)], 1), "col"
    )
    first_grad = norm_in_grad[:, :feature_count]
    second_grad = norm_in_grad[:, feature_count:]
    norm_part = jnp.stack(
        [
            jnp.sum(first_grad * normed, 0),
            jnp.sum(first_grad, 0),
            jnp.sum(second_grad * normed, 0),
            jnp.sum(second_grad, 0),
        ],
        0,
    )
    combined = norm_params[0] * first_grad + norm_params[2] * second_grad
    back_sums = lax.psum((jnp.sum(combined, 1), jnp.sum(combined * normed, 1)), "row")
    grad_all = cot_all.astype(jnp.float32) + rstd * (
        combined - back_sums[0][:, None] / D - normed * back_sums[1][:, None] / D
    )
    input_grad = lax.dynamic_slice_in_dim(grad_all, col_index * local_count, local_count, 0).astype(
        jnp.bfloat16
    )
    norm_grad, qkv_grad, proj_grad, up_grad, down_grad = lax.psum(
        (norm_part, qkv_grad, grad_cat[:attn_width], up_grad, grad_cat[attn_width:]), "dp"
    )
    norm_new, norm_first_new, norm_second_new = adam_update(
        norm_params, norm_first, norm_second, norm_grad, 0.0
    )
    qkv_new, qkv_first_new, qkv_second_new = adam_update(
        qkv_weight, qkv_first, qkv_second, qkv_grad, decay_rate
    )
    proj_new, proj_first_new, proj_second_new = adam_update(
        proj_weight, proj_first, proj_second, proj_grad, decay_rate
    )
    up_new, up_first_new, up_second_new = adam_update(
        up_weight, up_first, up_second, up_grad, decay_rate
    )
    down_new, down_first_new, down_second_new = adam_update(
        down_weight, down_first, down_second, down_grad, decay_rate
    )
    return (
        output,
        input_grad,
        norm_grad,
        qkv_grad,
        proj_grad,
        up_grad,
        down_grad,
        norm_new,
        qkv_new,
        proj_new,
        up_new,
        down_new,
        norm_first_new,
        norm_second_new,
        qkv_first_new,
        qkv_second_new,
        proj_first_new,
        proj_second_new,
        up_first_new,
        up_second_new,
        down_first_new,
        down_second_new,
    )


def solution(mesh):
    placed = (
        P(("dp", "col"), "row"),
        P(("dp", "col"), "row"),
        P("dp", None),
        P(None, "row"),
        P("row", "col"),
        P("col", "row"),
        P("row", "col"),
        P("col", "row"),
        P(None, "row"),
        P(None, "row"),
        P("row", "col"),
        P("row", "col"),
        P("col", "row"),
        P("col", "row"),
        P("row", "col"),
        P("row", "col"),
        P("col", "row"),
        P("col", "row"),
    )
    return jax.shard_map(
        on_device,
        mesh=mesh,
        in_specs=placed,
        out_specs=(
            P(("dp", "col"), "row"),
            P(("dp", "col"), "row"),
            P(None, "row"),
            P("row", "col"),
            P("col", "row"),
            P("row", "col"),
            P("col", "row"),
            P(None, "row"),
            P("row", "col"),
            P("col", "row"),
            P("row", "col"),
            P("col", "row"),
            P(None, "row"),
            P(None, "row"),
            P("row", "col"),
            P("row", "col"),
            P("col", "row"),
            P("col", "row"),
            P("row", "col"),
            P("row", "col"),
            P("col", "row"),
            P("col", "row"),
        ),
        check_vma=False,
    )
```

profile of v0, /device:TPU:0, one launch (start us, length us, event | category | flops | bytes accessed | tf_op | source)
XLA Modules:
  0.0 1250.0 jit_solution(12887507174771581139)
XLA Ops:
  7.3 13.2 %all_gather.21 = bf16[2048,192]{0,1:T(8,128)(2,1)S(1)} all-gather(bf16[1024,192]{0,1:T(8,128)(2,1)} %param.19), channel_id=1, replica_groups=mesh['dp'=4,'row'=4,'col'=2] {'col'}, dimensions={0}, use_global_device_ids=true | all-gather | bytes 1179648 | tf_op jit(solution)/shard_map/all_gather | solution.py:172
  22.1 7.8 convolution_bitcast_fusion
  30.9 10.9 all_gather.18
  42.0 20.0 %all-reduce.1 = (f32[2048]{0:T(1024)S(1)}, f32[2048]{0:T(1024)S(1)}) all-reduce(f32[2048]{0:T(1024)S(1)} %get-tuple-element.85, f32[2048]{0:T(1024)S(1)} %get-tuple-element.84), channel_id=1, replica_groups=mesh['dp'=4,'row'=4,'col'=2] {'row'}, use_global_device_ids=true, to_apply=%region_3.0 | all-reduce | flops 4096 | bytes 32768 | tf_op jit(solution)/shard_map/psum | solution.py:177
  65.7 11.2 pad_maximum_fusion
  80.2 214.4 %reduce-scatter.8.cloned.1.call-done = f32[512,1920]{0,1:T(8,128)} async-done(((f32[2048,1920]{0,1:T(8,128)}), f32[512,1920]{0,1:T(8,128)}) %reduce-scatter.8.cloned.1.call-update) | async-done | bytes 3932176 | tf_op jit(solution)/shard_map/reduce_scatter | solution.py:216
  295.8 366.3 %reduce-scatter.4.cloned.1.call-done = f32[512,2688]{0,1:T(8,128)} async-done(((f32[2048,2688]{0,1:T(8,128)}), f32[512,2688]{0,1:T(8,128)}) %reduce-scatter.4.cloned.1.call-update) | async-done | bytes 5505040 | tf_op jit(solution)/shard_map/reduce_scatter | solution.py:190
  666.5 7.8 fusion.1
  674.3 4.8 multiply_reduce_fusion.3
  679.2 4.0 multiply_convert_fusion
  688.0 4.9 fusion.9
  693.8 24.0 %all-gather.5.cloned.1.call-done = bf16[2048,384]{0,1:T(8,128)(2,1)} async-done(((bf16[512,384]{0,1:T(8,128)(2,1)}), bf16[2048,384]{0,1:T(8,128)(2,1)}) %all-gather.5.cloned.1.call-update) | async-done | bytes 1572880 | tf_op jit(solution)/shard_map/all_gather | solution.py:209
  717.8 2.8 constant_dynamic-update-slice_fusion.1
  720.6 87.5 %all-gather.9.cloned.1.call-done = bf16[2048,1152]{0,1:T(8,128)(2,1)} async-done(((bf16[512,1152]{0,1:T(8,128)(2,1)}), bf16[2048,1152]{0,1:T(8,128)(2,1)}) %all-gather.9.cloned.1.call-update) | async-done | bytes 4718608 | tf_op jit(solution)/shard_map/all_gather | solution.py:232
  808.1 5.0 fusion.65
  813.1 110.2 %all-gather.7.cloned.1.call-done = bf16[2048,1536]{0,1:T(8,128)(2,1)} async-done(((bf16[512,1536]{0,1:T(8,128)(2,1)}), bf16[2048,1536]{0,1:T(8,128)(2,1)}) %all-gather.7.cloned.1.call-update) | async-done | bytes 6291472 | tf_op jit(solution)/shard_map/all_gather | solution.py:210
  923.3 6.5 constant_dynamic-update-slice_fusion
  929.8 6.7 fusion.74
  938.4 99.8 %all-gather.11.cloned.1.call-done = bf16[2048,1536]{0,1:T(8,128)(2,1)} async-done(((bf16[512,1536]{0,1:T(8,128)(2,1)}), bf16[2048,1536]{0,1:T(8,128)(2,1)}) %all-gather.11.cloned.1.call-update) | async-done | bytes 6291472 | tf_op jit(solution)/shard_map/all_gather | solution.py:233
  1038.2 6.0 fusion.66
  1045.5 3.5 fusion.48
  1049.0 4.2 fusion.44
  1053.2 2.1 pad_maximum_fusion.1
  1056.3 6.4 fusion.39
  1062.7 54.8 %all-reduce.8.cloned.1.call-done = (f32[192,1152]{1,0:T(8,128)}, f32[384,192]{0,1:T(8,128)}, f32[192,1536]{1,0:T(8,128)}, f32[1536,192]{0,1:T(8,128)}) async-done(((f32[192,1152]{1,0:T(8,128)}, f32[384,192]{0,1:T(8,128)}, f32[192,1536]{1,0:T(8,128)}, f32[1536,192]{0,1:T(8,128)}), (f32[192,1152]{1,0:T(8,128)}, f32[384,192]{0,1:T(8,128)}, f32[192,1536]{1,0:T(8,128)}, ...) | async-done | bytes 3538960 | tf_op jit(solution)/shard_map/psum | solution.py:260
  1117.6 2.2 multiply_subtract_fusion.3
  1119.8 4.5 multiply_subtract_fusion
  1124.4 2.4 multiply_subtract_fusion.1
  1129.5 76.3 %all-reduce.6.cloned.1.call-done = f32[2048,384]{0,1:T(8,128)} async-done(((f32[2048,384]{0,1:T(8,128)}), f32[2048,384]{0,1:T(8,128)}) %all-reduce.6.cloned.1.call-update) | async-done | bytes 3145744 | tf_op jit(solution)/shard_map/psum | solution.py:238
  1205.8 4.1 multiply_reduce_fusion.1
  1210.0 18.9 %all-reduce = (f32[2048]{0:T(1024)S(1)}, f32[2048]{0:T(1024)S(1)}) all-reduce(f32[2048]{0:T(1024)S(1)} %get-tuple-element.82, f32[2048]{0:T(1024)S(1)} %get-tuple-element.83), channel_id=1, replica_groups=mesh['dp'=4,'row'=4,'col'=2] {'row'}, use_global_device_ids=true, to_apply=%region_13.14 | all-reduce | flops 4096 | bytes 32768 | tf_op jit(solution)/shard_map/psum | solution.py:253
  1228.9 6.1 psum.75
  (178 shorter events, 36.2 us)
Async XLA Ops:
  7.2 13.2 %copy-start.7 = (f32[1536,192]{0,1:T(8,128)S(1)}, f32[1536,192]{0,1:T(8,128)}, u32[]{:S(2)}) copy-start(f32[1536,192]{0,1:T(8,128)} %param.25) | copy-start | bytes 3538948
  7.2 13.3 %copy-start.20 = (f32[384,192]{0,1:T(8,128)S(1)}, f32[384,192]{0,1:T(8,128)}, u32[]{:S(2)}) copy-start(f32[384,192]{0,1:T(8,128)} %param.23) | copy-start | bytes 884740
  7.2 287.4 %reduce-scatter.8.cloned.1.call-start = ((), (), s32[]{:S(2)}) async-start(), calls=%async_computation.7 | async-start | bytes 19660800 | tf_op jit(solution)/shard_map/reduce_scatter | solution.py:216
  20.4 9.4 copy-start.4
  29.9 32.1 %copy-start.41 = (f32[4,192]{1,0:T(4,128)S(1)}, f32[4,192]{1,0:T(4,128)}, u32[]{:S(2)}) copy-start(f32[4,192]{1,0:T(4,128)} %param.21) | copy-start | bytes 9220
  29.9 32.2 %copy-start.2 = (f32[192,1152]{1,0:T(8,128)S(1)}, f32[192,1152]{1,0:T(8,128)}, u32[]{:S(2)}) copy-start(f32[192,1152]{1,0:T(8,128)} %param.22) | copy-start | bytes 2654212
  29.9 632.2 %reduce-scatter.4.cloned.1.call-start = ((), (), s32[]{:S(2)}) async-start(), calls=%async_computation.3 | async-start | bytes 27525120 | tf_op jit(solution)/shard_map/reduce_scatter | solution.py:190
  76.9 640.9 %all-gather.5.cloned.1.call-start = ((), (), s32[]{:S(2)}) async-start(), calls=%async_computation.4 | async-start | bytes 1966080 | tf_op jit(solution)/shard_map/all_gather | solution.py:209
  679.1 128.9 %all-gather.9.cloned.1.call-start = ((), (), s32[]{:S(2)}) async-start(), calls=%async_computation.8 | async-start | bytes 5898240 | tf_op jit(solution)/shard_map/all_gather | solution.py:232
  679.2 6.3 slice-start
  687.9 235.3 %all-gather.7.cloned.1.call-start = ((), (), s32[]{:S(2)}) async-start(), calls=%async_computation.5 | async-start | bytes 7864320 | tf_op jit(solution)/shard_map/all_gather | solution.py:210
  692.9 345.3 %all-gather.11.cloned.1.call-start = ((), (), s32[]{:S(2)}) async-start(), calls=%async_computation.9 | async-start | bytes 7864320 | tf_op jit(solution)/shard_map/all_gather | solution.py:233
  693.5 114.6 %copy-start.38 = (f32[1,192]{1,0:T(1,128)S(1)}, f32[1,192]{1,0:T(1,128)}, u32[]{:S(2)}) copy-start(f32[1,192]{1,0:T(1,128)} %copy-done.37) | copy-start | bytes 2308
  693.5 114.6 %copy-start.47 = (f32[1,192]{1,0:T(1,128)S(1)}, f32[1,192]{1,0:T(1,128)}, u32[]{:S(2)}) copy-start(f32[1,192]{1,0:T(1,128)} %copy-done.46) | copy-start | bytes 2308
  693.5 424.0 %all-reduce.8.cloned.1.call-start = ((), (), s32[]{:S(2)}) async-start(), calls=%async_computation.11 | async-start | bytes 7077888 | tf_op jit(solution)/shard_map/psum | solution.py:260
  813.1 116.7 %copy-start.5 = (bf16[2048,192]{0,1:T(8,128)(2,1)S(1)}, bf16[2048,192]{0,1:T(8,128)(2,1)}, u32[]{:S(2)}) copy-start(bf16[2048,192]{0,1:T(8,128)(2,1)} %copy-done.4) | copy-start | bytes 2359300
  936.5 101.8 %copy-start.40 = (f32[1,192]{1,0:T(1,128)S(1)}, f32[1,192]{1,0:T(1,128)}, u32[]{:S(2)}) copy-start(f32[1,192]{1,0:T(1,128)} %copy-done.39) | copy-start | bytes 2308
  936.5 101.7 %copy-start.45 = (f32[1,192]{1,0:T(1,128)S(1)}, f32[1,192]{1,0:T(1,128)}, u32[]{:S(2)}) copy-start(f32[1,192]{1,0:T(1,128)} %copy-done.44) | copy-start | bytes 2308
  1044.3 4.7 copy-start.1
  1044.3 161.5 %all-reduce.6.cloned.1.call-start = ((), (), s32[]{:S(2)}) async-start(), calls=%async_computation.10 | async-start | bytes 6291456 | tf_op jit(solution)/shard_map/psum | solution.py:238
  1055.3 182.4 %reduce-scatter.6.cloned.1.call-start = ((), (), s32[]{:S(2)}) async-start(), calls=%async_computation.6 | async-start | bytes 2359296 | tf_op jit(solution)/shard_map/reduce_scatter | solution.py:213
  1062.7 54.9 %copy-start.21 = (f32[384,192]{0,1:T(8,128)S(1)}, f32[384,192]{0,1:T(8,128)}, u32[]{:S(2)}) copy-start(f32[384,192]{0,1:T(8,128)} %param.23) | copy-start | bytes 884740
  1062.7 54.9 %copy-start.28 = (f32[384,192]{0,1:T(8,128)S(1)}, f32[384,192]{0,1:T(8,128)}, u32[]{:S(2)}) copy-start(f32[384,192]{0,1:T(8,128)} %param.30) | copy-start | bytes 884740
  1119.8 4.6 copy-start.10
  1119.8 4.6 copy-start.23
  1119.8 4.6 copy-start.24
  1129.5 105.4 %copy-start.42 = (f32[4,192]{1,0:T(4,128)S(1)}, f32[4,192]{1,0:T(4,128)}, u32[]{:S(2)}) copy-start(f32[4,192]{1,0:T(4,128)} %param.21) | copy-start | bytes 9220
  1129.5 105.4 %copy-start.49 = (f32[4,192]{1,0:T(4,128)S(1)}, f32[4,192]{1,0:T(4,128)}, u32[]{:S(2)}) copy-start(f32[4,192]{1,0:T(4,128)} %param.26) | copy-start | bytes 9220
  1129.5 105.4 %copy-start.50 = (f32[4,192]{1,0:T(4,128)S(1)}, f32[4,192]{1,0:T(4,128)}, u32[]{:S(2)}) copy-start(f32[4,192]{1,0:T(4,128)} %param.27) | copy-start | bytes 9220
  1129.5 106.1 %copy-start.6 = (bf16[2048,192]{0,1:T(8,128)(2,1)S(1)}, bf16[2048,192]{0,1:T(8,128)(2,1)}, u32[]{:S(2)}) copy-start(bf16[2048,192]{0,1:T(8,128)(2,1)} %copy-done.4) | copy-start | bytes 2359300
  1210.0 27.7 %copy-start.17 = (bf16[1024,192]{0,1:T(8,128)(2,1)S(1)}, bf16[1024,192]{0,1:T(8,128)(2,1)}, u32[]{:S(2)}) copy-start(bf16[1024,192]{0,1:T(8,128)(2,1)} %param.18) | copy-start | bytes 1179652
  1235.0 4.8 copy-start.43
  (30 other events, 55.4 us)
Sparse Core Ops, SparseCore 0:
  30.0 264.5 reduce-scatter.7
  297.0 365.1 reduce-scatter.3
  679.3 38.5 all-gather.4
  719.8 88.2 all-gather.8
  809.5 113.7 all-gather.6
  924.7 113.4 all-gather.10
  1044.4 73.0 all-reduce.7
  1119.9 85.9 all-reduce.5
  1208.1 26.1 reduce-scatter.5
where the time goes:
time: 1250 us
  waiting for transfers between devices  1030 us (82%)
  blocking collectives  69 us (6%)
  matrix products  62.5 us (5%)
  other arithmetic  41.8 us (3%)
  local copies, waits for them, and re-layouts  27.1 us (2%)
  between operations  14.5 us (1%)
    reduce_scatter x1, waiting for transfers between devices, on_device(): lax.psum_scatter(jnp.concatenate([dot32(first_in, qkv16), dot32(second_in...  366 us
    reduce_scatter x1, waiting for transfers between devices, on_device(): lax.psum_scatter(dot_cols(cot_all, proj_cat), 'row', scatter_dimension=0,...  214 us
    all_gather x1, waiting for transfers between devices, on_device(): lax.all_gather(active, 'row', axis=0, tiled=True)  110 us
    all_gather x1, waiting for transfers between devices, on_device(): lax.all_gather(hidden_grad, 'row', axis=0, tiled=True)  99.8 us
    all_gather x1, waiting for transfers between devices, on_device(): lax.all_gather(packed_grad, 'row', axis=0, tiled=True)  87.5 us
    psum x1, waiting for transfers between devices, on_device(): lax.psum(jnp.concatenate([dot_cols(packed_all, qkv16), dot_cols(hidden_al...  76.3 us
    psum x1, waiting for transfers between devices, on_device(): lax.psum((norm_part, qkv_grad, grad_cat[:attn_width], up_grad, grad_cat[a...  54.8 us
  transfers between devices with their start and end apart: 9, of which 8 were waited for; matrix products, arithmetic and copies ran while one was open for 7% of the time, Pallas kernels for 0%

commit v1 on v0

--- a/solution.py
+++ b/solution.py
@@ -235,8 +235,11 @@
     qkv_grad = dot_rows(first_in, packed_all)
     up_grad = dot_rows(second_in, hidden_all)
     feature_count = first_in.shape[1]
-    norm_in_grad = lax.psum(
-        jnp.concatenate([dot_cols(packed_all, qkv16), dot_cols(hidden_all, up16)], 1), "col"
+    norm_in_grad = jnp.sum(
+        lax.all_gather(
+            jnp.concatenate([dot_cols(packed_all, qkv16), dot_cols(hidden_all, up16)], 1), "col"
+        ),
+        axis=0,
     )
     first_grad = norm_in_grad[:, :feature_count]
     second_grad = norm_in_grad[:, feature_count:]

time: 1250 us -> 1300 us (1.040)
  waiting for transfers between devices: 1030 us -> 1050 us
    all_gather x0 -> x1, waiting for transfers between devices: none -> 80 us  [on_device(): lax.all_gather(jnp.concatenate([dot_cols(packed_all, qkv16), dot_cols(hid...]
    psum x1 -> x0, waiting for transfers between devices: 76.3 us -> none  [on_device(): lax.psum(jnp.concatenate([dot_cols(packed_all, qkv16), dot_cols(hidden_al...]
    reduce_scatter x1, waiting for transfers between devices: 0.01 us -> 17 us  [on_device(): lax.psum_scatter(dot32(act_cat, proj_cat), 'col', scatter_dimension=0, ti...]
  transfers between devices with their start and end apart: 9 -> 9, of which waited for: 8 -> 9; matrix products, arithmetic and copies ran while one was open for 7% -> 7% of each run, Pallas kernels for 0% -> 0%
where the time goes in v1:
time: 1300 us; the launch traced here: 1290 us
  waiting for transfers between devices  1050 us (81%)
  blocking collectives  69.2 us (5%)
  matrix products  63 us (5%)
  other arithmetic  53.7 us (4%)
  local copies, waits for them, and re-layouts  37.4 us (3%)
  between operations  14.7 us (1%)
    reduce_scatter x1, waiting for transfers between devices, on_device(): lax.psum_scatter(jnp.concatenate([dot32(first_in, qkv16), dot32(second_in...  366 us
    reduce_scatter x1, waiting for transfers between devices, on_device(): lax.psum_scatter(dot_cols(cot_all, proj_cat), 'row', scatter_dimension=0,...  214 us
    all_gather x1, waiting for transfers between devices, on_device(): lax.all_gather(active, 'row', axis=0, tiled=True)  110 us
    all_gather x1, waiting for transfers between devices, on_device(): lax.all_gather(hidden_grad, 'row', axis=0, tiled=True)  99.8 us
    all_gather x1, waiting for transfers between devices, on_device(): lax.all_gather(packed_grad, 'row', axis=0, tiled=True)  87.5 us
    all_gather x1, waiting for transfers between devices, on_device(): lax.all_gather(jnp.concatenate([dot_cols(packed_all, qkv16), dot_cols(hid...  80 us
    psum x1, waiting for transfers between devices, on_device(): lax.psum((norm_part, qkv_grad, grad_cat[:attn_width], up_grad, grad_cat[a...  54.3 us
  transfers between devices with their start and end apart: 9, of which 9 were waited for; matrix products, arithmetic and copies ran while one was open for 7% of the time, Pallas kernels for 0%

profile of v1, /device:TPU:0, one launch (start us, length us, event | category | flops | bytes accessed | tf_op | source)
XLA Modules:
  0.0 1293.3 jit_solution(4184695304295103280)
XLA Ops:
  7.3 13.2 %all_gather.27 = bf16[2048,192]{0,1:T(8,128)(2,1)S(1)} all-gather(bf16[1024,192]{0,1:T(8,128)(2,1)} %param.19), channel_id=1, replica_groups=mesh['dp'=4,'row'=4,'col'=2] {'col'}, dimensions={0}, use_global_device_ids=true | all-gather | bytes 1179648 | tf_op jit(solution)/shard_map/all_gather | solution.py:172
  22.1 7.8 convolution_bitcast_fusion
  30.9 10.9 all_gather.24
  42.0 20.0 %all-reduce.1 = (f32[2048]{0:T(1024)S(1)}, f32[2048]{0:T(1024)S(1)}) all-reduce(f32[2048]{0:T(1024)S(1)} %get-tuple-element.85, f32[2048]{0:T(1024)S(1)} %get-tuple-element.84), channel_id=1, replica_groups=mesh['dp'=4,'row'=4,'col'=2] {'row'}, use_global_device_ids=true, to_apply=%region_3.0 | all-reduce | flops 4096 | bytes 32768 | tf_op jit(solution)/shard_map/psum | solution.py:177
  65.7 11.2 pad_maximum_fusion
  80.2 214.4 %reduce-scatter.8.cloned.1.call-done = f32[512,1920]{0,1:T(8,128)} async-done(((f32[2048,1920]{0,1:T(8,128)}), f32[512,1920]{0,1:T(8,128)}) %reduce-scatter.8.cloned.1.call-update) | async-done | bytes 3932176 | tf_op jit(solution)/shard_map/reduce_scatter | solution.py:216
  295.8 366.3 %reduce-scatter.4.cloned.1.call-done = f32[512,2688]{0,1:T(8,128)} async-done(((f32[2048,2688]{0,1:T(8,128)}), f32[512,2688]{0,1:T(8,128)}) %reduce-scatter.4.cloned.1.call-update) | async-done | bytes 5505040 | tf_op jit(solution)/shard_map/reduce_scatter | solution.py:190
  666.5 7.8 fusion.1
  674.3 4.8 multiply_reduce_fusion.3
  679.2 4.0 multiply_convert_fusion
  688.0 4.9 fusion.9
  693.8 24.0 %all-gather.7.cloned.1.call-done = bf16[2048,384]{0,1:T(8,128)(2,1)} async-done(((bf16[512,384]{0,1:T(8,128)(2,1)}), bf16[2048,384]{0,1:T(8,128)(2,1)}) %all-gather.7.cloned.1.call-update) | async-done | bytes 1572880 | tf_op jit(solution)/shard_map/all_gather | solution.py:209
  717.8 2.8 constant_dynamic-update-slice_fusion.1
  720.6 87.5 %all-gather.11.cloned.1.call-done = bf16[2048,1152]{0,1:T(8,128)(2,1)} async-done(((bf16[512,1152]{0,1:T(8,128)(2,1)}), bf16[2048,1152]{0,1:T(8,128)(2,1)}) %all-gather.11.cloned.1.call-update) | async-done | bytes 4718608 | tf_op jit(solution)/shard_map/all_gather | solution.py:232
  808.1 5.0 fusion.65
  813.1 110.2 %all-gather.9.cloned.1.call-done = bf16[2048,1536]{0,1:T(8,128)(2,1)} async-done(((bf16[512,1536]{0,1:T(8,128)(2,1)}), bf16[2048,1536]{0,1:T(8,128)(2,1)}) %all-gather.9.cloned.1.call-update) | async-done | bytes 6291472 | tf_op jit(solution)/shard_map/all_gather | solution.py:210
  923.3 6.5 constant_dynamic-update-slice_fusion
  929.8 6.7 fusion.74
  938.4 99.8 %all-gather.13.cloned.1.call-done = bf16[2048,1536]{0,1:T(8,128)(2,1)} async-done(((bf16[512,1536]{0,1:T(8,128)(2,1)}), bf16[2048,1536]{0,1:T(8,128)(2,1)}) %all-gather.13.cloned.1.call-update) | async-done | bytes 6291472 | tf_op jit(solution)/shard_map/all_gather | solution.py:233
  1038.3 6.0 fusion.66
  1045.4 6.7 fusion.39
  1053.3 3.6 fusion.48
  1056.9 4.2 fusion.44
  1063.2 54.3 %all-reduce.5.cloned.1.call-done = (f32[192,1152]{1,0:T(8,128)}, f32[384,192]{0,1:T(8,128)}, f32[192,1536]{1,0:T(8,128)}, f32[1536,192]{0,1:T(8,128)}) async-done(((f32[192,1152]{1,0:T(8,128)}, f32[384,192]{0,1:T(8,128)}, f32[192,1536]{1,0:T(8,128)}, f32[1536,192]{0,1:T(8,128)}), (f32[192,1152]{1,0:T(8,128)}, f32[384,192]{0,1:T(8,128)}, f32[192,1536]{1,0:T(8,128)}, ...) | async-done | bytes 3538960 | tf_op jit(solution)/shard_map/psum | solution.py:263
  1119.8 4.5 multiply_subtract_fusion
  1129.1 17.0 %reduce-scatter.6.cloned.1.call-done = f32[1024,192]{0,1:T(8,128)} async-done(((f32[2048,192]{0,1:T(8,128)}), f32[1024,192]{0,1:T(8,128)}) %reduce-scatter.6.cloned.1.call-update) | async-done | bytes 786448 | tf_op jit(solution)/shard_map/reduce_scatter | solution.py:213
  1148.1 80.0 %all-gather.15.cloned.1.call-done = f32[4096,384]{0,1:T(8,128)} async-done(((f32[2048,384]{0,1:T(8,128)}), f32[4096,384]{0,1:T(8,128)}) %all-gather.15.cloned.1.call-update) | async-done | bytes 6291472 | tf_op jit(solution)/shard_map/all_gather | solution.py:239
  1228.1 9.4 reshape.317
  1237.4 11.9 reduce_sum.105
  1249.4 4.2 multiply_reduce_fusion.1
  1253.6 6.4 psum.67
  1260.0 18.7 %all-reduce = (f32[2048]{0:T(1024)S(1)}, f32[2048]{0:T(1024)S(1)}) all-reduce(f32[2048]{0:T(1024)S(1)} %get-tuple-element.82, f32[2048]{0:T(1024)S(1)} %get-tuple-element.83), channel_id=1, replica_groups=mesh['dp'=4,'row'=4,'col'=2] {'row'}, use_global_device_ids=true, to_apply=%region_13.14 | all-reduce | flops 4096 | bytes 32768 | tf_op jit(solution)/shard_map/psum | solution.py:256
  (180 shorter events, 43.7 us)
Async XLA Ops:
  7.2 13.2 %copy-start.7 = (f32[1536,192]{0,1:T(8,128)S(1)}, f32[1536,192]{0,1:T(8,128)}, u32[]{:S(2)}) copy-start(f32[1536,192]{0,1:T(8,128)} %param.25) | copy-start | bytes 3538948
  7.2 13.3 %copy-start.19 = (f32[384,192]{0,1:T(8,128)S(1)}, f32[384,192]{0,1:T(8,128)}, u32[]{:S(2)}) copy-start(f32[384,192]{0,1:T(8,128)} %param.23) | copy-start | bytes 884740
  7.2 287.4 %reduce-scatter.8.cloned.1.call-start = ((), (), s32[]{:S(2)}) async-start(), calls=%async_computation.7 | async-start | bytes 19660800 | tf_op jit(solution)/shard_map/reduce_scatter | solution.py:216
  20.4 9.4 copy-start.4
  29.9 32.1 %copy-start.41 = (f32[4,192]{1,0:T(4,128)S(1)}, f32[4,192]{1,0:T(4,128)}, u32[]{:S(2)}) copy-start(f32[4,192]{1,0:T(4,128)} %param.21) | copy-start | bytes 9220
  29.9 32.2 %copy-start.2 = (f32[192,1152]{1,0:T(8,128)S(1)}, f32[192,1152]{1,0:T(8,128)}, u32[]{:S(2)}) copy-start(f32[192,1152]{1,0:T(8,128)} %param.22) | copy-start | bytes 2654212
  29.9 632.2 %reduce-scatter.4.cloned.1.call-start = ((), (), s32[]{:S(2)}) async-start(), calls=%async_computation.3 | async-start | bytes 27525120 | tf_op jit(solution)/shard_map/reduce_scatter | solution.py:190
  76.9 640.9 %all-gather.7.cloned.1.call-start = ((), (), s32[]{:S(2)}) async-start(), calls=%async_computation.4 | async-start | bytes 1966080 | tf_op jit(solution)/shard_map/all_gather | solution.py:209
  679.1 128.9 %all-gather.11.cloned.1.call-start = ((), (), s32[]{:S(2)}) async-start(), calls=%async_computation.8 | async-start | bytes 5898240 | tf_op jit(solution)/shard_map/all_gather | solution.py:232
  679.2 6.3 slice-start
  687.9 235.3 %all-gather.9.cloned.1.call-start = ((), (), s32[]{:S(2)}) async-start(), calls=%async_computation.5 | async-start | bytes 7864320 | tf_op jit(solution)/shard_map/all_gather | solution.py:210
  692.9 345.3 %all-gather.13.cloned.1.call-start = ((), (), s32[]{:S(2)}) async-start(), calls=%async_computation.9 | async-start | bytes 7864320 | tf_op jit(solution)/shard_map/all_gather | solution.py:233
  693.5 114.6 %copy-start.38 = (f32[1,192]{1,0:T(1,128)S(1)}, f32[1,192]{1,0:T(1,128)}, u32[]{:S(2)}) copy-start(f32[1,192]{1,0:T(1,128)} %copy-done.37) | copy-start | bytes 2308
  693.5 114.6 %copy-start.47 = (f32[1,192]{1,0:T(1,128)S(1)}, f32[1,192]{1,0:T(1,128)}, u32[]{:S(2)}) copy-start(f32[1,192]{1,0:T(1,128)} %copy-done.46) | copy-start | bytes 2308
  693.6 424.0 %all-reduce.5.cloned.1.call-start = ((), (), s32[]{:S(2)}) async-start(), calls=%async_computation.11 | async-start | bytes 7077888 | tf_op jit(solution)/shard_map/psum | solution.py:263
  813.1 116.7 %copy-start.5 = (bf16[2048,192]{0,1:T(8,128)(2,1)S(1)}, bf16[2048,192]{0,1:T(8,128)(2,1)}, u32[]{:S(2)}) copy-start(bf16[2048,192]{0,1:T(8,128)(2,1)} %copy-done.4) | copy-start | bytes 2359300
  936.5 101.8 %copy-start.40 = (f32[1,192]{1,0:T(1,128)S(1)}, f32[1,192]{1,0:T(1,128)}, u32[]{:S(2)}) copy-start(f32[1,192]{1,0:T(1,128)} %copy-done.39) | copy-start | bytes 2308
  936.5 101.7 %copy-start.45 = (f32[1,192]{1,0:T(1,128)S(1)}, f32[1,192]{1,0:T(1,128)}, u32[]{:S(2)}) copy-start(f32[1,192]{1,0:T(1,128)} %copy-done.44) | copy-start | bytes 2308
  1044.3 101.8 %reduce-scatter.6.cloned.1.call-start = ((), (), s32[]{:S(2)}) async-start(), calls=%async_computation.6 | async-start | bytes 2359296 | tf_op jit(solution)/shard_map/reduce_scatter | solution.py:213
  1052.1 4.8 copy-start.1
  1052.1 175.9 %all-gather.15.cloned.1.call-start = ((), (), s32[]{:S(2)}) async-start(), calls=%async_computation.10 | async-start | bytes 9437184 | tf_op jit(solution)/shard_map/all_gather | solution.py:239
  1063.2 54.4 %copy-start.20 = (f32[384,192]{0,1:T(8,128)S(1)}, f32[384,192]{0,1:T(8,128)}, u32[]{:S(2)}) copy-start(f32[384,192]{0,1:T(8,128)} %param.23) | copy-start | bytes 884740
  1063.2 54.4 %copy-start.28 = (f32[384,192]{0,1:T(8,128)S(1)}, f32[384,192]{0,1:T(8,128)}, u32[]{:S(2)}) copy-start(f32[384,192]{0,1:T(8,128)} %param.30) | copy-start | bytes 884740
  1119.8 4.6 copy-start.10
  1119.8 4.6 copy-start.22
  1119.8 4.6 copy-start.23
  1127.2 18.9 %copy-start.16 = (bf16[1024,192]{0,1:T(8,128)(2,1)S(1)}, bf16[1024,192]{0,1:T(8,128)(2,1)}, u32[]{:S(2)}) copy-start(bf16[1024,192]{0,1:T(8,128)(2,1)} %param.18) | copy-start | bytes 1179652
  1249.4 29.4 %copy-start.42 = (f32[4,192]{1,0:T(4,128)S(1)}, f32[4,192]{1,0:T(4,128)}, u32[]{:S(2)}) copy-start(f32[4,192]{1,0:T(4,128)} %param.21) | copy-start | bytes 9220
  1249.4 29.4 %copy-start.49 = (f32[4,192]{1,0:T(4,128)S(1)}, f32[4,192]{1,0:T(4,128)}, u32[]{:S(2)}) copy-start(f32[4,192]{1,0:T(4,128)} %param.26) | copy-start | bytes 9220
  1249.4 29.4 %copy-start.50 = (f32[4,192]{1,0:T(4,128)S(1)}, f32[4,192]{1,0:T(4,128)}, u32[]{:S(2)}) copy-start(f32[4,192]{1,0:T(4,128)} %param.27) | copy-start | bytes 9220
  1249.4 30.0 %copy-start.6 = (bf16[2048,192]{0,1:T(8,128)(2,1)S(1)}, bf16[2048,192]{0,1:T(8,128)(2,1)}, u32[]{:S(2)}) copy-start(bf16[2048,192]{0,1:T(8,128)(2,1)} %copy-done.4) | copy-start | bytes 2359300
  1260.0 23.8 %copy-start.43 = (f32[4,192]{1,0:T(4,128)}, f32[4,192]{1,0:T(4,128)S(1)}, u32[]{:S(2)}) copy-start(f32[4,192]{1,0:T(4,128)S(1)} %psum.67) | copy-start | bytes 9220
  (30 other events, 56.7 us)
Sparse Core Ops, SparseCore 0:
  30.0 264.5 reduce-scatter.7
  297.0 365.1 reduce-scatter.3
  679.3 38.4 all-gather.6
  719.8 88.2 all-gather.10
  809.5 113.7 all-gather.8
  924.7 113.4 all-gather.12
  1044.4 73.0 all-reduce.4
  1119.8 26.2 reduce-scatter.5
  1147.7 80.3 all-gather.14
